TPU v7x, 32 devices: a whole 2x2x4 slice. The times are simulated.
32 devices in a mesh: row: 4 (over y, core), col: 8 (over z, x).
Axes of the slice: x: 2, y: 2, z: 4, core: 2. Of those that a mesh axis runs over, the one named last changes fastest.
Arguments:
- front: float32 [12288, 12288], P('row', 'col'), may hold values from -6 to 6
- delayed: float32 [64, 12288], P('col', 'row'), may hold values from -6 to 6
- dest: int32 [64], P('col'), may hold values from 0 to 1023, as said below
- pivots: int32 [1024], replicated, may hold values from 0 to 12287, as said below
- pair_flags: int32 [1024], replicated, may hold values from 0 to 1, as said below
- linv: float32 [4, 256, 256], replicated, as said below
- dinv_diag: float32 [1024], replicated, may hold values from -0.1 to 0.1
- dinv_off: float32 [1024], replicated, may hold values from -0.08 to 0.08
Outputs:
- trailing: float32 [12288, 12288], P('row', 'col')
- factor: float32 [12288, 1024], P('row')
Inputs may be any that keep to these rules, and one draw needn't show every extreme that they name: Distinct front columns; slots p * 256 to (p + 1) * 256 - 1 are panel p's pivots. Each block of 1536 columns held by one index of col contains exactly 128 of them. `pair_flags`: A 1 at slot s joins slots s and s + 1 into one 2x2 block; no two 1s are adjacent and the last slot of a panel holds 0. `dest`: several delayed columns may share a slot. Of the 8 delayed columns held by one index of col, at most 2 go to pivot columns held by the same index of col. `linv`: each panel's matrix is unit lower triangular: ones on the diagonal, zeros above it.
All inputs are finite; a program needn't handle non-finite values.
Results may differ from a plain program's by a relative error of at most 0.00015.
Values sent between devices are 32-bit elements; how exact they have to be, the bound alone decides.
A program may use at most 192 MiB of HBM per device.

v0:
```python
import jax
import jax.numpy as jnp
from jax import lax
from jax.sharding import PartitionSpec as P

CAP = 2
precise = lax.Precision.HIGHEST


def broadcast(block, axis, holder):
    block = jnp.where(lax.axis_index(axis) == holder, block, jnp.zeros_like(block))
    return lax.psum(block, axis)


def pair_scale(scaled, pair_bits, diag_part, off_part):
    coupled = pair_bits.astype(jnp.float32) * off_part
    zero_col = jnp.zeros_like(scaled[:, :1])
    shifted_next = jnp.concatenate([scaled[:, 1:], zero_col], axis=1)
    shifted_prev = jnp.concatenate([zero_col, scaled[:, :-1]], axis=1)
    coupled_prev = jnp.concatenate([jnp.zeros_like(coupled[:1]), coupled[:-1]])
    return scaled * diag_part + shifted_next * coupled + shifted_prev * coupled_prev


def select_columns(matrix, wanted, anchor):
    block_width = matrix.shape[1]
    relative = wanted - anchor
    inside = (relative >= 0) & (relative < block_width)
    clipped = jnp.clip(relative, 0, block_width - 1)
    return jnp.where(inside[None, :], jnp.take(matrix, clipped, axis=1), 0.0)


def select_rows(matrix, wanted, anchor):
    block_height = matrix.shape[0]
    relative = wanted - anchor
    inside = (relative >= 0) & (relative < block_height)
    clipped = jnp.clip(relative, 0, block_height - 1)
    return jnp.where(inside[:, None], jnp.take(matrix, clipped, axis=0), 0.0)


def body(front, delayed, dest, pivots, pair_flags, linv, dinv_diag, dinv_off):
    col_count = lax.axis_size("col")
    rows_blk, cols_blk = front.shape
    row_start = lax.axis_index("row") * rows_blk
    col_start = lax.axis_index("col") * cols_blk
    panel_count = linv.shape[0]
    panel_width = linv.shape[1]
    slot_total = pivots.shape[0]
    slot_ids = jnp.arange(slot_total, dtype=jnp.int32)
    owner_ids = jnp.arange(col_count, dtype=jnp.int32)
    slot_hit = dest[:, None] == slot_ids[None, :]
    targets = jnp.sum(jnp.where(slot_hit, pivots[None, :], 0), axis=1)
    owners = targets // cols_blk
    within = targets - owners * cols_blk
    owner_hit = (owners[:, None] == owner_ids[None, :]).astype(jnp.int32)
    earlier = jnp.cumsum(owner_hit, axis=0) - owner_hit
    rank_in = jnp.sum(earlier * owner_hit, axis=1)
    slot_pos = jnp.arange(CAP, dtype=jnp.int32)
    placed = (owner_hit[:, :, None] > 0) & (rank_in[:, None, None] == slot_pos[None, None, :])
    send_vals = jnp.einsum("kos,kr->osr", placed.astype(jnp.float32), delayed, precision=precise)
    send_cols = jnp.sum(jnp.where(placed, within[:, None, None] + 1, 0), axis=0) - 1
    recv_vals, recv_cols = (
        lax.all_to_all(send_vals, "col", split_axis=0, concat_axis=0, tiled=True),
        lax.all_to_all(send_cols, "col", split_axis=0, concat_axis=0, tiled=True),
    )
    flat_vals = recv_vals.reshape(-1, rows_blk)
    flat_cols = recv_cols.reshape(-1)
    col_ids = jnp.arange(cols_blk, dtype=jnp.int32)
    col_hit = (flat_cols[:, None] == col_ids[None, :]).astype(jnp.float32)
    current = front + lax.dot_general(
        flat_vals, col_hit, (((0,), (0,)), ((), ())), precision=precise
    )
    factors = []
    piv_owner = pivots // cols_blk
    piv_hit = (piv_owner[:, None] == owner_ids[None, :]).astype(jnp.int32)
    piv_rank = jnp.sum((jnp.cumsum(piv_hit, axis=0) - piv_hit) * piv_hit, axis=1)
    per_owner = slot_total // col_count
    owned_here = piv_owner == lax.axis_index("col")
    rank_ids = jnp.arange(per_owner, dtype=jnp.int32)
    own_slots = jnp.sum(
        jnp.where(
            owned_here[None, :] & (piv_rank[None, :] == rank_ids[:, None]), slot_ids[None, :], 0
        ),
        axis=1,
    )
    compact = select_columns(current, pivots[own_slots], col_start)
    gathered = lax.all_gather(compact, "col", axis=1, tiled=True)
    every_panel = jnp.take(gathered, piv_owner * per_owner + piv_rank, axis=1)
    previous = []
    for panel_index in range(panel_count):
        offset = panel_index * panel_width
        panel_cols = every_panel[:, offset : offset + panel_width]
        for cols_before, rows_before in previous:
            panel_cols = panel_cols - lax.dot_general(
                cols_before,
                rows_before[offset : offset + panel_width],
                (((1,), (1,)), ((), ())),
                precision=precise,
            )
        finish_offset = panel_index * panel_width
        finish_scaled = jnp.dot(panel_cols, jnp.transpose(linv[panel_index]), precision=precise)
        finish_columns = pair_scale(
            finish_scaled,
            pair_flags[finish_offset : finish_offset + panel_width],
            dinv_diag[finish_offset : finish_offset + panel_width],
            dinv_off[finish_offset : finish_offset + panel_width],
        )
        root_row = col_start // rows_blk
        slice_start = jnp.clip(col_start - row_start, 0, rows_blk - cols_blk)
        root_piece = lax.dynamic_slice_in_dim(finish_scaled, slice_start, cols_blk, 0)
        col_scaled = broadcast(root_piece, "row", root_row)
        current = current - lax.dot_general(
            finish_columns, col_scaled, (((1,), (1,)), ((), ())), precision=precise
        )
        factors.append(finish_columns)
        if panel_index + 1 < panel_count:
            pivot_part = select_rows(finish_scaled, pivots, row_start)
            pivot_rows = lax.psum(pivot_part, "row")
            previous.append((finish_columns, pivot_rows))
    row_ids = row_start + jnp.arange(rows_blk, dtype=jnp.int32)
    row_in = jnp.any(row_ids[:, None] == pivots[None, :], axis=1)
    col_in = jnp.any((col_start + col_ids)[:, None] == pivots[None, :], axis=1)
    trailing = jnp.where(row_in[:, None] | col_in[None, :], 0.0, current)
    factor = jnp.concatenate(factors, axis=1)
    return (trailing, factor)


def solution(mesh):
    return jax.shard_map(
        body,
        mesh=mesh,
        in_specs=(P("row", "col"), P("col", "row"), P("col"), P(), P(), P(), P(), P()),
        out_specs=(P("row", "col"), P("row", None)),
        check_vma=False,
    )
```

profile of v0, /device:TPU:0, one launch (start us, length us, event | category | flops | bytes accessed | tf_op | source)
XLA Modules:
  0.0 721.7 jit_solution(9475887452106300543)
XLA Ops:
  9.2 7.3 %all-to-all-start.1 = ((s32[8,1,2]{2,1,0:T(1,128)}), s32[8,1,2]{2,1,0:T(1,128)S(1)}, u32[]{:S(2)}, u32[]{:S(2)}) async-start(s32[8,1,2]{2,1,0:T(1,128)} %copy.32), calls=%async_computation.1 | async-start | bytes 8192 | tf_op jit(solution)/shard_map/all_to_all | solution.py:63
  36.8 18.0 %convolution_add_fusion = f32[3072,1536]{1,0:T(8,128)} fusion(f32[3072,1536]{1,0:T(8,128)} %param.10, f32[16,3072]{1,0:T(8,128)S(1)} %reshape.189, s32[16]{0:T(128)S(1)} %eq.152), kind=kOutput, calls=%fused_computation.7 | convolution fusion | flops 910712832 | bytes 37945408 | tf_op jit(solution)/shard_map/dot_general | solution.py:69
  54.8 18.7 %copy.33 = f32[3072,1536]{0,1:T(8,128)} copy(f32[3072,1536]{1,0:T(8,128)} %convolution_add_fusion) | data formatting | bytes 37748736 | tf_op jit(solution)/shard_map/add | solution.py:69
  73.4 8.2 %gather_fusion.1 = f32[128,3072]{1,0:T(8,128)S(1)} fusion(f32[3072,1536]{0,1:T(8,128)} %copy.33, s32[1024]{0:T(1024)S(1)} %pad_clamp_fusion), kind=kCustom, calls=%fused_computation.4 | custom fusion | bytes 3146240 | tf_op jit(solution)/shard_map/jit(_take)/gather | solution.py:29
  84.1 173.5 %all-gather.2.cloned.1.call-done = f32[3072,1024]{0,1:T(8,128)} async-done(((f32[3072,128]{0,1:T(8,128)}), f32[3072,1024]{0,1:T(8,128)}) %all-gather.2.cloned.1.call-update) | async-done | bytes 12582928 | tf_op jit(solution)/shard_map/all_gather | solution.py:86
  257.6 16.5 %gather_fusion.2 = f32[1024,3072]{1,0:T(8,128)} fusion(f32[3072,1024]{0,1:T(8,128)} %all-gather.2.cloned.1.call-done, s32[1024]{0:T(1024)S(1)} %broadcast_clamp_fusion), kind=kCustom, calls=%fused_computation.5 | custom fusion | bytes 25169920 | tf_op jit(solution)/shard_map/jit(_take)/gather | solution.py:87
  274.1 12.6 %copy.34 = f32[1024,3072]{0,1:T(8,128)} copy(f32[1024,3072]{1,0:T(8,128)} %gather_fusion.2) | data formatting | bytes 25165824 | tf_op jit(solution)/shard_map/jit(_take)/gather | solution.py:87
  286.7 12.4 %select_bitcast_fusion = f32[3072,1024]{1,0:T(8,128)} fusion(f32[1024,3072]{0,1:T(8,128)} %copy.34, pred[1024]{0:T(1024)(128)(4,1)S(1)} %compare_and_fusion.2), kind=kLoop, calls=%fused_computation.9 | loop fusion | flops 3145728 | bytes 25166848 | tf_op jit(solution)/shard_map/jit(_take)/select_n | solution.py:87
  324.0 27.4 %all-reduce.14.cloned.1.call-done = f32[1024,256]{1,0:T(8,128)} async-done(((f32[1024,256]{1,0:T(8,128)}), f32[1024,256]{1,0:T(8,128)}) %all-reduce.14.cloned.1.call-update) | async-done | bytes 1048592 | tf_op jit(solution)/shard_map/psum | solution.py:117
  351.4 7.3 %convolution_subtract_fusion.5 = f32[3072,256]{1,0:T(8,128)S(1)} fusion(f32[3072,256]{0,1:T(8,128)S(1)} %multiply_add_fusion.3, f32[3072,1024]{1,0:T(8,128)} %select_bitcast_fusion, f32[1024,256]{1,0:T(8,128)} %all-reduce.14.cloned.1.call-done), kind=kOutput, calls=%fused_computation.17 | convolution fusion | flops 2416705536 | bytes 9699328 | tf_op jit(solution)/shard_map/dot_general | solution.py:93
  387.6 8.0 %convolution_subtract_fusion.4 = f32[3072,256]{1,0:T(8,128)} fusion(f32[3072,256]{0,1:T(8,128)S(1)} %multiply_add_fusion.3, f32[3072,1024]{1,0:T(8,128)} %select_bitcast_fusion, f32[1024,256]{1,0:T(8,128)S(1)} %copy-done.19), kind=kOutput, calls=%fused_computation.16 | convolution fusion | flops 2416705536 | bytes 9699328 | tf_op jit(solution)/shard_map/dot_general | solution.py:93
  397.3 8.3 %convolution_subtract_fusion.2 = f32[3072,256]{1,0:T(8,128)} fusion(f32[3072,256]{0,1:T(8,128)S(1)} %multiply_add_fusion.3, f32[3072,1024]{1,0:T(8,128)} %select_bitcast_fusion, f32[1024,256]{1,0:T(8,128)S(1)} %copy-done.19), kind=kOutput, calls=%fused_computation.14 | convolution fusion | flops 2416705536 | bytes 9699328 | tf_op jit(solution)/shard_map/dot_general | solution.py:93
  405.5 11.8 %all-reduce.16.cloned.1.call-done = f32[1024,256]{1,0:T(8,128)} async-done(((f32[1024,256]{1,0:T(8,128)}), f32[1024,256]{1,0:T(8,128)}) %all-reduce.16.cloned.1.call-update) | async-done | bytes 1048592 | tf_op jit(solution)/shard_map/psum | solution.py:117
  417.3 8.3 %convolution_subtract_fusion.3 = f32[3072,256]{1,0:T(8,128)S(1)} fusion(f32[3072,256]{1,0:T(8,128)} %convolution_subtract_fusion.4, f32[3072,256]{0,1:T(8,128)} %multiply_add_fusion.2, f32[1024,256]{1,0:T(8,128)} %all-reduce.16.cloned.1.call-done), kind=kOutput, calls=%fused_computation.15 | convolution fusion | flops 2416705536 | bytes 9699328 | tf_op jit(solution)/shard_map/dot_general | solution.py:93
  447.7 7.0 multiply_add_fusion.1
  457.2 8.1 %convolution_subtract_fusion.1 = f32[3072,256]{1,0:T(8,128)} fusion(f32[3072,256]{1,0:T(8,128)S(1)} %copy-done.16, f32[3072,256]{0,1:T(8,128)S(1)} %copy-done.8, f32[1024,256]{1,0:T(8,128)} %all-reduce.16.cloned.1.call-done), kind=kOutput, calls=%fused_computation.13 | convolution fusion | flops 2416705536 | bytes 9699328 | tf_op jit(solution)/shard_map/dot_general | solution.py:93
  465.3 19.0 %all-reduce.18.cloned.1.call-done = f32[1024,256]{1,0:T(8,128)} async-done(((f32[1024,256]{1,0:T(8,128)}), f32[1024,256]{1,0:T(8,128)}) %all-reduce.18.cloned.1.call-update) | async-done | bytes 1048592 | tf_op jit(solution)/shard_map/psum | solution.py:117
  484.4 8.3 %convolution_subtract_fusion = f32[3072,256]{1,0:T(8,128)S(1)} fusion(f32[3072,256]{1,0:T(8,128)} %convolution_subtract_fusion.1, f32[3072,256]{0,1:T(8,128)} %multiply_add_fusion.1, f32[1024,256]{1,0:T(8,128)} %all-reduce.18.cloned.1.call-done), kind=kOutput, calls=%fused_computation.12 | convolution fusion | flops 2416705536 | bytes 9699328 | tf_op jit(solution)/shard_map/dot_general | solution.py:93
  517.4 12.6 %copy.38 = f32[3072,1024]{1,0:T(8,128)} copy(f32[3072,1024]{0,1:T(8,128)} %pad_maximum_fusion) | data formatting | bytes 25165824
  530.0 90.6 %all-reduce.20.cloned.1.call-done = (f32[1536,256]{0,1:T(8,128)}, f32[1536,256]{0,1:T(8,128)}, f32[1536,256]{0,1:T(8,128)}, f32[1536,256]{0,1:T(8,128)}) async-done(((f32[1536,256]{0,1:T(8,128)}, f32[1536,256]{0,1:T(8,128)}, f32[1536,256]{0,1:T(8,128)}, f32[1536,256]{0,1:T(8,128)}), (f32[1536,256]{0,1:T(8,128)}, f32[1536,256]{0,1:T(8,128)}, f32[1536,256]{0,1:T(8,128)}, ...) | async-done | bytes 6291472 | tf_op jit(solution)/shard_map/psum | solution.py:12
  620.6 19.9 %fusion.44 = f32[3072,1536]{1,0:T(8,128)} fusion(f32[3072,256]{0,1:T(8,128)} %multiply_add_fusion.1, f32[1536,256]{0,1:T(8,128)} %get-tuple-element.11), kind=kOutput, calls=%fused_computation.119 | convolution fusion | flops 14495514624 | bytes 23592960 | tf_op jit(solution)/shard_map/dot_general | solution.py:111
  640.5 18.5 %fusion.43 = f32[3072,1536]{1,0:T(8,128)} fusion(f32[3072,256]{0,1:T(8,128)S(1)} %copy-done.10, f32[1536,256]{0,1:T(8,128)S(1)} %copy-done.18), kind=kOutput, calls=%fused_computation.118 | convolution fusion | flops 14495514624 | bytes 23592960 | tf_op jit(solution)/shard_map/dot_general | solution.py:111
  659.0 17.9 %fusion.42 = f32[3072,1536]{1,0:T(8,128)} fusion(f32[3072,256]{0,1:T(8,128)S(1)} %multiply_add_fusion.3, f32[1536,256]{0,1:T(8,128)S(1)} %copy-done.17), kind=kOutput, calls=%fused_computation.117 | convolution fusion | flops 14495514624 | bytes 23592960 | tf_op jit(solution)/shard_map/dot_general | solution.py:111
  676.9 38.1 %subtract_select_fusion = f32[3072,1536]{1,0:T(8,128)} fusion(f32[3072,1536]{1,0:T(8,128)} %fusion.44, f32[3072,1536]{1,0:T(8,128)} %fusion.43, f32[3072,1536]{1,0:T(8,128)} %convolution_add_fusion, f32[3072,1536]{1,0:T(8,128)} %fusion.42, f32[3072,256]{0,1:T(8,128)} %copy-done.15, f32[1536,256]{0,1:T(8,128)} %get-tuple-element.14, ...), kind=kOutput, calls=%fused_computation.6 | convolution fusion | flops 14523826176 | bytes 99095040 | tf_op jit(solution)/shard_map/dot_general | solution.py:111
  (126 shorter events, 129.0 us)
Async XLA Ops:
  7.2 9.3 %copy-start = (f32[8,3072]{1,0:T(8,128)S(1)}, f32[8,3072]{1,0:T(8,128)}, u32[]{:S(2)}) copy-start(f32[8,3072]{1,0:T(8,128)} %param.11) | copy-start | bytes 294916
  9.2 13.7 %all-to-all-start.1 = ((s32[8,1,2]{2,1,0:T(1,128)}), s32[8,1,2]{2,1,0:T(1,128)S(1)}, u32[]{:S(2)}, u32[]{:S(2)}) async-start(s32[8,1,2]{2,1,0:T(1,128)} %copy.32), calls=%async_computation.1 | async-start | bytes 8192 | tf_op jit(solution)/shard_map/all_to_all | solution.py:63
  22.9 13.8 %all-to-all-start = ((f32[8,2,3072]{2,1,0:T(2,128)}), f32[8,2,3072]{2,1,0:T(2,128)S(1)}, u32[]{:S(2)}, u32[]{:S(2)}) async-start(f32[8,2,3072]{2,1,0:T(2,128)} %copy.31), calls=%async_computation | async-start | bytes 393216 | tf_op jit(solution)/shard_map/all_to_all | solution.py:62
  28.9 228.7 %all-gather.2.cloned.1.call-start = ((), (), s32[]{:S(2)}) async-start(), calls=%async_computation.2 | async-start | bytes 14155776 | tf_op jit(solution)/shard_map/all_gather | solution.py:86
  81.7 2.3 copy-start.11
  81.7 2.3 copy-start.22
  83.2 268.2 %all-reduce.14.cloned.1.call-start = ((), (), s32[]{:S(2)}) async-start(), calls=%async_computation.3 | async-start | bytes 2097152 | tf_op jit(solution)/shard_map/psum | solution.py:117
  304.0 3.7 copy-start.6
  316.7 100.6 %all-reduce.16.cloned.1.call-start = ((), (), s32[]{:S(2)}) async-start(), calls=%async_computation.4 | async-start | bytes 2097152 | tf_op jit(solution)/shard_map/psum | solution.py:117
  316.9 5.4 copy-start.7
  380.4 103.9 %all-reduce.18.cloned.1.call-start = ((), (), s32[]{:S(2)}) async-start(), calls=%async_computation.5 | async-start | bytes 2097152 | tf_op jit(solution)/shard_map/psum | solution.py:117
  380.7 7.0 copy-start.19
  387.6 8.0 %copy-start.5 = (f32[3072,256]{0,1:T(8,128)S(1)}, f32[3072,256]{0,1:T(8,128)}, u32[]{:S(2)}) copy-start(f32[3072,256]{0,1:T(8,128)} %copy-done.4) | copy-start | bytes 9437188
  447.5 173.2 %all-reduce.20.cloned.1.call-start = ((), (), s32[]{:S(2)}) async-start(), calls=%async_computation.6 | async-start | bytes 12582912 | tf_op jit(solution)/shard_map/psum | solution.py:12
  447.7 7.1 copy-start.3
  447.7 8.7 %copy-start.16 = (f32[3072,256]{1,0:T(8,128)S(1)}, f32[3072,256]{1,0:T(8,128)}, u32[]{:S(2)}) copy-start(f32[3072,256]{1,0:T(8,128)} %convolution_subtract_fusion.2) | copy-start | bytes 9437188
  454.7 2.5 copy-start.8
  503.4 4.6 copy-start.13
  508.0 3.0 copy-start.9
  508.0 4.0 copy-start.14
  620.6 19.9 %copy-start.10 = (f32[3072,256]{0,1:T(8,128)S(1)}, f32[3072,256]{0,1:T(8,128)}, u32[]{:S(2)}) copy-start(f32[3072,256]{0,1:T(8,128)} %multiply_add_fusion.2) | copy-start | bytes 9437188
  620.6 19.9 %copy-start.18 = (f32[1536,256]{0,1:T(8,128)S(1)}, f32[1536,256]{0,1:T(8,128)}, u32[]{:S(2)}) copy-start(f32[1536,256]{0,1:T(8,128)} %get-tuple-element.12) | copy-start | bytes 4718596
  640.5 18.5 %copy-start.17 = (f32[1536,256]{0,1:T(8,128)S(1)}, f32[1536,256]{0,1:T(8,128)}, u32[]{:S(2)}) copy-start(f32[1536,256]{0,1:T(8,128)} %get-tuple-element.13) | copy-start | bytes 4718596
  676.9 38.1 %copy-start.1 = (f32[8,3072]{1,0:T(8,128)S(1)}, f32[8,3072]{1,0:T(8,128)}, u32[]{:S(2)}) copy-start(f32[8,3072]{1,0:T(8,128)} %param.11) | copy-start | bytes 294916
  (6 other events, 10.8 us)
Sparse Core Ops, SparseCore 0:
  83.3 174.2 all-gather.1
  316.8 34.4 all-reduce.13
  380.5 36.7 all-reduce.15
  447.6 36.7 all-reduce.17
  500.5 120.0 all-reduce.19
where the time goes:
time: 728 us; the launch traced here: 722 us
  waiting for transfers between devices  329 us (45%)
  matrix products  178 us (24%)
  local copies, waits for them, and re-layouts  124 us (17%)
  other arithmetic  61.7 us (8%)
  starting transfers between devices  14.6 us (2%)
  between operations  14.4 us (2%)
    all_gather x1, waiting for transfers between devices, body(): gathered = lax.all_gather(compact, 'col', axis=1, tiled=True)  174 us
    dot_general x4, matrix products, body(): lax.dot_general(finish_columns, col_scaled, (((1,), (1,)), ((), ())), pre...  94.3 us
    psum x1, waiting for transfers between devices, broadcast(): return lax.psum(block, axis)  90.6 us
    psum x3, waiting for transfers between devices, body(): pivot_rows = lax.psum(pivot_part, 'row')  58.2 us
    dot_general x6, matrix products, body(): lax.dot_general(cols_before, rows_before[offset:offset + panel_width], ((...  48.4 us
    gather x2, local copies, waits for them, and re-layouts, body(): every_panel = jnp.take(gathered, piv_owner * per_owner + piv_rank, axis=1)  29.1 us
    unnamed x47, local copies, waits for them, and re-layouts  21.9 us
    add x4, other arithmetic, pair_scale(): scaled * diag_part + shifted_next * coupled + shifted_prev * coupled_prev  20.7 us
  transfers between devices with their start and end apart: 7, of which 6 were waited for; matrix products, arithmetic and copies ran while one was open for 11% of the time, Pallas kernels for 0%

commit v1 on v0

--- a/solution.py
+++ b/solution.py
@@ -114,7 +114,11 @@
         factors.append(finish_columns)
         if panel_index + 1 < panel_count:
             pivot_part = select_rows(finish_scaled, pivots, row_start)
-            pivot_rows = lax.psum(pivot_part, "row")
+            pivot_rows = pivot_part
+            for hop in (1, 2):
+                pivot_rows = pivot_rows + lax.ppermute(
+                    pivot_rows, "row", [(dev, dev ^ hop) for dev in range(4)]
+                )
             previous.append((finish_columns, pivot_rows))
     row_ids = row_start + jnp.arange(rows_blk, dtype=jnp.int32)
     row_in = jnp.any(row_ids[:, None] == pivots[None, :], axis=1)

time: 728 us -> 714 us (0.981)
  other arithmetic: 61.7 us -> 52.1 us
  local copies, waits for them, and re-layouts: 124 us -> 115 us
    ppermute x0 -> x6, waiting for transfers between devices: none -> 64.3 us  [body(): lax.ppermute(pivot_rows, 'row', [(dev, dev ^ hop) for dev in range(4)])]
    psum x3 -> x0, waiting for transfers between devices: 58.2 us -> none  [body(): pivot_rows = lax.psum(pivot_part, 'row')]
    add x4, other arithmetic: 20.7 us -> 7.58 us  [pair_scale(): scaled * diag_part + shifted_next * coupled + shifted_prev * coupled_prev]
    slice x4, local copies, waits for them, and re-layouts: 14.2 us -> 6.67 us  [pair_scale(): shifted_next = jnp.concatenate([scaled[:, 1:], zero_col], axis=1)]
    dot_general x6, matrix products: 48.4 us -> 40.9 us  [body(): lax.dot_general(cols_before, rows_before[offset:offset + panel_width], ((...]
  transfers between devices with their start and end apart: 7 -> 10, of which waited for: 6 -> 7; matrix products, arithmetic and copies ran while one was open for 11% -> 8% of each run, Pallas kernels for 0% -> 0%
where the time goes in v1:
time: 714 us; the launch traced here: 707 us
  waiting for transfers between devices  333 us (47%)
  matrix products  173 us (24%)
  local copies, waits for them, and re-layouts  115 us (16%)
  other arithmetic  52.1 us (7%)
  starting transfers between devices  18.3 us (3%)
  between operations  15.1 us (2%)
    all_gather x1, waiting for transfers between devices, body(): gathered = lax.all_gather(compact, 'col', axis=1, tiled=True)  174 us
    dot_general x4, matrix products, body(): lax.dot_general(finish_columns, col_scaled, (((1,), (1,)), ((), ())), pre...  94.3 us
    psum x1, waiting for transfers between devices, broadcast(): return lax.psum(block, axis)  88.4 us
    ppermute x6, waiting for transfers between devices, body(): lax.ppermute(pivot_rows, 'row', [(dev, dev ^ hop) for dev in range(4)])  64.3 us
    dot_general x6, matrix products, body(): lax.dot_general(cols_before, rows_before[offset:offset + panel_width], ((...  40.9 us
    gather x2, local copies, waits for them, and re-layouts, body(): every_panel = jnp.take(gathered, piv_owner * per_owner + piv_rank, axis=1)  29.1 us
    gather x3, local copies, waits for them, and re-layouts, select_rows(): return jnp.where(inside[:, None], jnp.take(matrix, clipped, axis=0), 0.0)  20.2 us
    dot_general x4, matrix products, body(): jnp.dot(panel_cols, jnp.transpose(linv[panel_index]), precision=precise)  20 us
  transfers between devices with their start and end apart: 10, of which 7 were waited for; matrix products, arithmetic and copies ran while one was open for 8% of the time, Pallas kernels for 0%

profile of v1, /device:TPU:0, one launch (start us, length us, event | category | flops | bytes accessed | tf_op | source)
XLA Modules:
  0.0 706.9 jit_solution(11838608188345294501)
XLA Ops:
  9.2 7.3 %all-to-all-start.1 = ((s32[8,1,2]{2,1,0:T(1,128)}), s32[8,1,2]{2,1,0:T(1,128)S(1)}, u32[]{:S(2)}, u32[]{:S(2)}) async-start(s32[8,1,2]{2,1,0:T(1,128)} %copy.32), calls=%async_computation.1 | async-start | bytes 8192 | tf_op jit(solution)/shard_map/all_to_all | solution.py:63
  36.8 18.0 %convolution_add_fusion = f32[3072,1536]{1,0:T(8,128)} fusion(f32[3072,1536]{1,0:T(8,128)} %param.10, f32[16,3072]{1,0:T(8,128)S(1)} %reshape.189, s32[16]{0:T(128)S(1)} %eq.152), kind=kOutput, calls=%fused_computation.7 | convolution fusion | flops 910712832 | bytes 37945408 | tf_op jit(solution)/shard_map/dot_general | solution.py:69
  54.8 18.6 %copy.33 = f32[3072,1536]{0,1:T(8,128)} copy(f32[3072,1536]{1,0:T(8,128)} %convolution_add_fusion) | data formatting | bytes 37748736 | tf_op jit(solution)/shard_map/add | solution.py:69
  73.4 8.2 %gather_fusion.1 = f32[128,3072]{1,0:T(8,128)S(1)} fusion(f32[3072,1536]{0,1:T(8,128)} %copy.33, s32[1024]{0:T(1024)S(1)} %pad_clamp_fusion), kind=kCustom, calls=%fused_computation.4 | custom fusion | bytes 3146240 | tf_op jit(solution)/shard_map/jit(_take)/gather | solution.py:29
  83.4 174.1 %all-gather.2.cloned.1.call-done = f32[3072,1024]{0,1:T(8,128)} async-done(((f32[3072,128]{0,1:T(8,128)}), f32[3072,1024]{0,1:T(8,128)}) %all-gather.2.cloned.1.call-update) | async-done | bytes 12582928 | tf_op jit(solution)/shard_map/all_gather | solution.py:86
  257.5 16.5 %gather_fusion.2 = f32[1024,3072]{1,0:T(8,128)} fusion(f32[3072,1024]{0,1:T(8,128)} %all-gather.2.cloned.1.call-done, s32[1024]{0:T(1024)S(1)} %broadcast_clamp_fusion), kind=kCustom, calls=%fused_computation.5 | custom fusion | bytes 25169920 | tf_op jit(solution)/shard_map/jit(_take)/gather | solution.py:87
  274.1 12.6 %copy.34 = f32[1024,3072]{0,1:T(8,128)} copy(f32[1024,3072]{1,0:T(8,128)} %gather_fusion.2) | data formatting | bytes 25165824 | tf_op jit(solution)/shard_map/jit(_take)/gather | solution.py:87
  286.7 12.4 %select_bitcast_fusion = f32[3072,1024]{1,0:T(8,128)} fusion(f32[1024,3072]{0,1:T(8,128)} %copy.34, pred[1024]{0:T(1024)(128)(4,1)S(1)} %compare_and_fusion.2), kind=kLoop, calls=%fused_computation.9 | loop fusion | flops 3145728 | bytes 25166848 | tf_op jit(solution)/shard_map/jit(_take)/select_n | solution.py:87
  306.6 7.0 gather_fusion.3
  326.5 19.8 %collective-permute-done.1 = f32[1024,256]{1,0:T(8,128)S(1)} collective-permute-done((f32[1024,256]{1,0:T(8,128)S(1)}, f32[1024,256]{1,0:T(8,128)S(1)}, u32[]{:S(2)}, u32[]{:S(2)}) %collective-permute-start.1) | collective-permute-done | bytes 1048608 | tf_op jit(solution)/shard_map/ppermute | solution.py:119
  346.4 7.6 %convolution_subtract_fusion.2 = f32[3072,256]{1,0:T(8,128)S(1)} fusion(f32[3072,256]{0,1:T(8,128)S(1)} %multiply_add_fusion.3, f32[3072,1024]{1,0:T(8,128)} %select_bitcast_fusion, f32[1024,256]{1,0:T(8,128)S(1)} %add.184), kind=kOutput, calls=%fused_computation.17 | convolution fusion | flops 2416705536 | bytes 9699328 | tf_op jit(solution)/shard_map/dot_general | solution.py:93
  363.2 6.7 gather_fusion.4
  381.0 21.0 %collective-permute-done.3 = f32[1024,256]{1,0:T(8,128)S(1)} collective-permute-done((f32[1024,256]{1,0:T(8,128)S(1)}, f32[1024,256]{1,0:T(8,128)S(1)}, u32[]{:S(2)}, u32[]{:S(2)}) %collective-permute-start.3) | collective-permute-done | bytes 1048608 | tf_op jit(solution)/shard_map/ppermute | solution.py:119
  407.5 7.5 %fusion.2 = f32[3072,256]{1,0:T(8,128)S(1)} fusion(f32[3072,256]{1,0:T(8,128)S(1)} %fusion.11, f32[3072,256]{0,1:T(8,128)S(1)} %multiply_add_fusion.3, f32[3072,1024]{1,0:T(8,128)} %select_bitcast_fusion, f32[1024,256]{1,0:T(8,128)} %copy-done.16), kind=kOutput, calls=%fused_computation.16 | convolution fusion | flops 2417491968 | bytes 12845056 | tf_op jit(solution)/shard_map/dot_general | solution.py:93
  424.1 6.5 gather_fusion.5
  432.3 7.3 %fusion.8 = f32[3072,256]{1,0:T(8,128)S(1)} fusion(f32[3072,256]{0,1:T(8,128)} %copy-done.5, f32[1024,256]{1,0:T(8,128)} %copy-done.17), kind=kOutput, calls=%fused_computation.38 | convolution fusion | flops 2415919104 | bytes 6553600 | tf_op jit(solution)/shard_map/dot_general | solution.py:93
  445.9 20.8 %collective-permute-done.5 = f32[1024,256]{1,0:T(8,128)S(1)} collective-permute-done((f32[1024,256]{1,0:T(8,128)S(1)}, f32[1024,256]{1,0:T(8,128)S(1)}, u32[]{:S(2)}, u32[]{:S(2)}) %collective-permute-start.5) | collective-permute-done | bytes 1048608 | tf_op jit(solution)/shard_map/ppermute | solution.py:119
  472.3 7.5 %fusion.1 = f32[3072,256]{1,0:T(8,128)S(1)} fusion(f32[3072,256]{1,0:T(8,128)S(1)} %fusion.6, f32[3072,256]{1,0:T(8,128)S(1)} %fusion.8, f32[3072,256]{0,1:T(8,128)S(1)} %multiply_add_fusion.3, f32[3072,1024]{1,0:T(8,128)} %select_bitcast_fusion, f32[1024,256]{1,0:T(8,128)} %copy-done.16), kind=kOutput, calls=%fused_computation.14 | convolution fusion | flops 2418278400 | bytes 15990784 | tf_op jit(solution)/shard_map/dot_general | solution.py:93
  504.2 12.6 %copy.38 = f32[3072,1024]{1,0:T(8,128)} copy(f32[3072,1024]{0,1:T(8,128)} %pad_maximum_fusion) | data formatting | bytes 25165824
  516.9 88.4 %all-reduce.11.cloned.1.call-done = (f32[1536,256]{0,1:T(8,128)}, f32[1536,256]{0,1:T(8,128)}, f32[1536,256]{0,1:T(8,128)}, f32[1536,256]{0,1:T(8,128)}) async-done(((f32[1536,256]{0,1:T(8,128)}, f32[1536,256]{0,1:T(8,128)}, f32[1536,256]{0,1:T(8,128)}, f32[1536,256]{0,1:T(8,128)}), (f32[1536,256]{0,1:T(8,128)}, f32[1536,256]{0,1:T(8,128)}, f32[1536,256]{0,1:T(8,128)}, ...) | async-done | bytes 6291472 | tf_op jit(solution)/shard_map/psum | solution.py:12
  605.2 19.9 %fusion.50 = f32[3072,1536]{1,0:T(8,128)} fusion(f32[3072,256]{0,1:T(8,128)} %copy-done.11, f32[1536,256]{0,1:T(8,128)} %get-tuple-element.11), kind=kOutput, calls=%fused_computation.123 | convolution fusion | flops 14495514624 | bytes 23592960 | tf_op jit(solution)/shard_map/dot_general | solution.py:111
  625.1 18.3 %fusion.49 = f32[3072,1536]{1,0:T(8,128)} fusion(f32[3072,256]{0,1:T(8,128)S(1)} %copy-done.7, f32[1536,256]{0,1:T(8,128)S(1)} %copy-done.19), kind=kOutput, calls=%fused_computation.122 | convolution fusion | flops 14495514624 | bytes 23592960 | tf_op jit(solution)/shard_map/dot_general | solution.py:111
  643.4 17.9 %fusion.48 = f32[3072,1536]{1,0:T(8,128)} fusion(f32[3072,256]{0,1:T(8,128)S(1)} %multiply_add_fusion.3, f32[1536,256]{0,1:T(8,128)S(1)} %copy-done.18), kind=kOutput, calls=%fused_computation.121 | convolution fusion | flops 14495514624 | bytes 23592960 | tf_op jit(solution)/shard_map/dot_general | solution.py:111
  661.4 38.2 %subtract_select_fusion = f32[3072,1536]{1,0:T(8,128)} fusion(f32[3072,1536]{1,0:T(8,128)} %fusion.50, f32[3072,1536]{1,0:T(8,128)} %fusion.49, f32[3072,1536]{1,0:T(8,128)} %convolution_add_fusion, f32[3072,1536]{1,0:T(8,128)} %fusion.48, f32[3072,256]{0,1:T(8,128)} %copy-done.13, f32[1536,256]{0,1:T(8,128)} %get-tuple-element.14, ...), kind=kOutput, calls=%fused_computation.6 | convolution fusion | flops 14523826176 | bytes 99095040 | tf_op jit(solution)/shard_map/dot_general | solution.py:111
  (134 shorter events, 117.0 us)
Async XLA Ops:
  7.2 9.3 %copy-start = (f32[8,3072]{1,0:T(8,128)S(1)}, f32[8,3072]{1,0:T(8,128)}, u32[]{:S(2)}) copy-start(f32[8,3072]{1,0:T(8,128)} %param.11) | copy-start | bytes 294916
  9.2 13.7 %all-to-all-start.1 = ((s32[8,1,2]{2,1,0:T(1,128)}), s32[8,1,2]{2,1,0:T(1,128)S(1)}, u32[]{:S(2)}, u32[]{:S(2)}) async-start(s32[8,1,2]{2,1,0:T(1,128)} %copy.32), calls=%async_computation.1 | async-start | bytes 8192 | tf_op jit(solution)/shard_map/all_to_all | solution.py:63
  22.9 13.8 %all-to-all-start = ((f32[8,2,3072]{2,1,0:T(2,128)}), f32[8,2,3072]{2,1,0:T(2,128)S(1)}, u32[]{:S(2)}, u32[]{:S(2)}) async-start(f32[8,2,3072]{2,1,0:T(2,128)} %copy.31), calls=%async_computation | async-start | bytes 393216 | tf_op jit(solution)/shard_map/all_to_all | solution.py:62
  28.9 228.7 %all-gather.2.cloned.1.call-start = ((), (), s32[]{:S(2)}) async-start(), calls=%async_computation.2 | async-start | bytes 14155776 | tf_op jit(solution)/shard_map/all_gather | solution.py:86
  83.1 522.2 %all-reduce.11.cloned.1.call-start = ((), (), s32[]{:S(2)}) async-start(), calls=%async_computation.3 | async-start | bytes 12582912 | tf_op jit(solution)/shard_map/psum | solution.py:12
  303.9 18.6 %copy-start.2 = (f32[3072,256]{0,1:T(8,128)}, f32[3072,256]{0,1:T(8,128)S(1)}, u32[]{:S(2)}) copy-start(f32[3072,256]{0,1:T(8,128)S(1)} %fusion.3) | copy-start | bytes 9437188
  306.6 9.5 %copy-start.20 = (f32[1024]{0:T(1024)S(1)}, f32[1024]{0:T(1024)}, u32[]{:S(2)}) copy-start(f32[1024]{0:T(1024)} %param.17) | copy-start | bytes 12292
  306.6 9.5 %copy-start.21 = (s32[1024]{0:T(1024)S(1)}, s32[1024]{0:T(1024)}, u32[]{:S(2)}) copy-start(s32[1024]{0:T(1024)} %param.14) | copy-start | bytes 12292
  306.6 9.5 %copy-start.22 = (f32[1024]{0:T(1024)S(1)}, f32[1024]{0:T(1024)}, u32[]{:S(2)}) copy-start(f32[1024]{0:T(1024)} %param.16) | copy-start | bytes 12292
  316.1 3.0 collective-permute-start
  321.0 25.3 %collective-permute-start.1 = (f32[1024,256]{1,0:T(8,128)S(1)}, f32[1024,256]{1,0:T(8,128)S(1)}, u32[]{:S(2)}, u32[]{:S(2)}) collective-permute-start(f32[1024,256]{1,0:T(8,128)S(1)} %fusion.71), channel_id=1, source_target_pairs={{0,16},{8,24},{16,0},{24,8},{1,17},{9,25},{17,1},{25,9},{2,18},{10... | collective-permute-start | bytes 3145736 | tf_op jit(solution)/shard_map/ppermute | solution.py:119
  346.4 7.6 %copy-start.16 = (f32[1024,256]{1,0:T(8,128)}, f32[1024,256]{1,0:T(8,128)S(1)}, u32[]{:S(2)}) copy-start(f32[1024,256]{1,0:T(8,128)S(1)} %add.184) | copy-start | bytes 3145732
  371.6 3.9 collective-permute-start.2
  376.4 25.6 %collective-permute-start.3 = (f32[1024,256]{1,0:T(8,128)S(1)}, f32[1024,256]{1,0:T(8,128)S(1)}, u32[]{:S(2)}, u32[]{:S(2)}) collective-permute-start(f32[1024,256]{1,0:T(8,128)S(1)} %fusion.70), channel_id=1, source_target_pairs={{0,16},{8,24},{16,0},{24,8},{1,17},{9,25},{17,1},{25,9},{2,18},{10... | collective-permute-start | bytes 3145736 | tf_op jit(solution)/shard_map/ppermute | solution.py:119
  381.0 26.5 %copy-start.5 = (f32[3072,256]{0,1:T(8,128)}, f32[3072,256]{0,1:T(8,128)S(1)}, u32[]{:S(2)}) copy-start(f32[3072,256]{0,1:T(8,128)S(1)} %multiply_add_fusion.2) | copy-start | bytes 9437188
  402.1 5.4 copy-start.17
  432.2 7.4 %copy-start.3 = (f32[3072,256]{0,1:T(8,128)S(1)}, f32[3072,256]{0,1:T(8,128)}, u32[]{:S(2)}) copy-start(f32[3072,256]{0,1:T(8,128)} %fusion.17) | copy-start | bytes 9437188
  432.2 8.2 %collective-permute-start.4 = (f32[1024,256]{1,0:T(8,128)S(1)}, f32[1024,256]{1,0:T(8,128)S(1)}, u32[]{:S(2)}, u32[]{:S(2)}) collective-permute-start(f32[1024,256]{1,0:T(8,128)S(1)} %select_select_fusion), channel_id=1, source_target_pairs={{0,8},{8,0},{16,24},{24,16},{1,9},{9,1},{17,25},{25,17},{2,10},{10... | collective-permute-start | bytes 3145736 | tf_op jit(solution)/shard_map/ppermute | solution.py:119
  441.2 25.5 %collective-permute-start.5 = (f32[1024,256]{1,0:T(8,128)S(1)}, f32[1024,256]{1,0:T(8,128)S(1)}, u32[]{:S(2)}, u32[]{:S(2)}) collective-permute-start(f32[1024,256]{1,0:T(8,128)S(1)} %fusion.69), channel_id=1, source_target_pairs={{0,16},{8,24},{16,0},{24,8},{1,17},{9,25},{17,1},{25,9},{2,18},{10... | collective-permute-start | bytes 3145736 | tf_op jit(solution)/shard_map/ppermute | solution.py:119
  445.9 26.4 %copy-start.11 = (f32[3072,256]{0,1:T(8,128)}, f32[3072,256]{0,1:T(8,128)S(1)}, u32[]{:S(2)}) copy-start(f32[3072,256]{0,1:T(8,128)S(1)} %multiply_add_fusion.1) | copy-start | bytes 9437188
  605.2 19.9 %copy-start.7 = (f32[3072,256]{0,1:T(8,128)S(1)}, f32[3072,256]{0,1:T(8,128)}, u32[]{:S(2)}) copy-start(f32[3072,256]{0,1:T(8,128)} %copy-done.5) | copy-start | bytes 9437188
  605.2 19.9 %copy-start.19 = (f32[1536,256]{0,1:T(8,128)S(1)}, f32[1536,256]{0,1:T(8,128)}, u32[]{:S(2)}) copy-start(f32[1536,256]{0,1:T(8,128)} %get-tuple-element.12) | copy-start | bytes 4718596
  625.1 18.3 %copy-start.18 = (f32[1536,256]{0,1:T(8,128)S(1)}, f32[1536,256]{0,1:T(8,128)}, u32[]{:S(2)}) copy-start(f32[1536,256]{0,1:T(8,128)} %get-tuple-element.13) | copy-start | bytes 4718596
  661.4 38.2 %copy-start.1 = (f32[8,3072]{1,0:T(8,128)S(1)}, f32[8,3072]{1,0:T(8,128)}, u32[]{:S(2)}) copy-start(f32[8,3072]{1,0:T(8,128)} %param.11) | copy-start | bytes 294916
  (9 other events, 23.9 us)
Sparse Core Ops, SparseCore 0:
  83.2 174.2 all-gather.1
  487.4 117.8 all-reduce.10
